TPU v7x, 32 devices: a whole 2x2x4 slice. The times are simulated.
32 devices in a mesh: row: 4 (over y, x), col: 8 (over z, core).
Axes of the slice: x: 2, y: 2, z: 4, core: 2. Of those that a mesh axis runs over, the one named last changes fastest.
Arguments:
- panel_factor: bfloat16 [128, 20480], P('row', 'col'), may hold values from -0.5 to 0.5
- diag_inverse: bfloat16 [128, 128], P('col'), may hold values from -0.5 to 0.5
- panel_rhs: bfloat16 [128, 18432], P('col', 'row'), may hold values from -6 to 6
- trail_rhs: bfloat16 [18432, 20480], P('row', 'col'), may hold values from -6 to 6
- forward_field: bfloat16 [18432, 20480], P('row', 'col'), may hold values from -6 to 6
- pivot: int32 [128], replicated, may hold values from 0 to 127, each once
- panel_harmonic: int32 [2, 128], replicated, may hold values from 0 to 90
- trail_harmonic: int32 [2, 20480], P(None, 'col'), may hold values from 0 to 90
Outputs:
- panel_adjoint: bfloat16 [128, 18432], P(None, 'row')
- trail_update: bfloat16 [18432, 20480], P('row', 'col')
- eps_grad: float32 [36864], P(('row', 'col'))
All inputs are finite; a program needn't handle non-finite values.
Results may differ from a plain program's by a relative error of at most 0.0039.
Values may be sent and summed in bfloat16 or wider, within the bound.
No kernel may reach another device: no remote copies, remote signals or barrier semaphores. Data moves between devices by JAX's collectives and lax.ppermute only.
A program may use at most 128 MiB of HBM per device.

v0:
```python
import math

import jax
import jax.numpy as jnp
from jax import lax
from jax.sharding import PartitionSpec as P

NB = 128
S = 18432
ORDERS = 91
DPITCH = 192
NDIAG = 36864


def per_device(
    panel_factor,
    diag_inverse,
    panel_rhs,
    trail_rhs,
    forward_field,
    pivot,
    panel_harmonic,
    trail_harmonic,
):
    contract_first = (((0,), (0,)), ((), ()))
    inverse_all, rhs_all = (
        lax.all_gather(diag_inverse, "col", axis=0, tiled=True),
        lax.all_gather(panel_rhs, "col", axis=0, tiled=True),
    )
    panel_adjoint = lax.dot_general(
        inverse_all, rhs_all, contract_first, preferred_element_type=jnp.float32
    ).astype(jnp.bfloat16)
    update = lax.dot_general(
        panel_adjoint,
        lax.all_gather(panel_factor, "row", axis=0, tiled=True),
        contract_first,
        preferred_element_type=jnp.float32,
    )
    trail_update = (trail_rhs.astype(jnp.float32) - update).astype(jnp.bfloat16)
    correlation = jnp.dot(panel_adjoint, forward_field, preferred_element_type=jnp.float32)
    harmonic_rows = panel_harmonic[:, pivot]
    correlation = lax.psum_scatter(correlation, "row", scatter_dimension=0, tiled=True)
    row_count = NB // lax.axis_size("row")
    first_row = lax.axis_index("row") * row_count
    harmonic_rows = lax.dynamic_slice_in_dim(harmonic_rows, first_row, row_count, 1)
    delta_x = harmonic_rows[0][:, None] - trail_harmonic[0][None, :] + (ORDERS - 1)
    delta_y = harmonic_rows[1][:, None] - trail_harmonic[1][None, :] + (ORDERS - 1)
    cell_index = (delta_x * DPITCH + delta_y).reshape(-1)
    partial_grad = jax.ops.segment_sum(correlation.reshape(-1), cell_index, num_segments=NDIAG)
    gradient = lax.psum_scatter(partial_grad, ("row", "col"), scatter_dimension=0, tiled=True)
    eps_grad = gradient * jnp.float32(1.0 / math.sqrt(S * NB))
    return (panel_adjoint, trail_update, eps_grad)


def solution(mesh):
    placed = (
        P("row", "col"),
        P("col", None),
        P("col", "row"),
        P("row", "col"),
        P("row", "col"),
        P(),
        P(),
        P(None, "col"),
    )
    return jax.shard_map(
        per_device,
        mesh=mesh,
        in_specs=placed,
        out_specs=(P(None, "row"), P("row", "col"), P(("row", "col"))),
        check_vma=False,
    )
```

profile of v0, /device:TPU:0, one launch (start us, length us, event | category | flops | bytes accessed | tf_op | source)
XLA Modules:
  0.0 638.5 jit_solution(8719130069794366491)
XLA Ops:
  7.2 0.0 all-gather.2.cloned.1.call-start
  7.2 0.7 all-gather.2.cloned.1.call-update
  7.9 0.0 reduce-scatter.2.cloned.1.call-start
  7.9 15.9 %all_gather.9 = bf16[128,128]{1,0:T(8,128)(2,1)S(1)} all-gather(bf16[16,128]{1,0:T(8,128)(2,1)} %param.9), channel_id=1, replica_groups=mesh['row'=4,'col'=8] {'col'}, dimensions={0}, use_global_device_ids=true | all-gather | bytes 36864 | tf_op jit(solution)/shard_map/all_gather | solution.py:27
  23.9 11.3 %all-gather.2.cloned.1.call-done = bf16[128,4608]{1,0:T(8,128)(2,1)} async-done(((bf16[16,4608]{1,0:T(8,128)(2,1)}), bf16[128,4608]{1,0:T(8,128)(2,1)}) %all-gather.2.cloned.1.call-update) | async-done | bytes 1179664 | tf_op jit(solution)/shard_map/all_gather | solution.py:28
  35.2 1.8 convolution_convert_fusion
  36.9 0.0 copy-start
  36.9 10.9 %fusion.2 = f32[128,2560]{1,0:T(8,128)} fusion(bf16[128,4608]{1,0:T(8,128)(2,1)S(1)} %convolution_convert_fusion, bf16[4608,2560]{1,0:T(8,128)(2,1)} %param.12), kind=kOutput, calls=%fused_computation.15 | convolution fusion | flops 3019898880 | bytes 26083328 | tf_op jit(solution)/shard_map/dot_general | solution.py:40
  47.9 0.0 copy-start.3
  47.9 0.0 copy-start.4
  47.9 0.0 copy-start.2
  47.9 0.0 copy-start.1
  47.9 0.0 reduce-scatter.2.cloned.1.call-update
  47.9 0.0 all-reduce.3.cloned.1.call-start
  48.0 0.6 copy-done.3
  48.5 0.1 copy.13
  48.7 0.0 copy-done.4
  48.7 0.6 gather_fusion
  49.3 0.2 slice_reduce_fusion.1
  49.5 0.0 copy-done.2
  49.5 0.1 slice_reduce_fusion.3
  49.6 0.1 add_add_fusion
  49.8 0.0 copy-done.1
  49.8 15.9 %all_gather.11 = bf16[128,2560]{1,0:T(8,128)(2,1)S(1)} all-gather(bf16[32,2560]{1,0:T(8,128)(2,1)S(1)} %copy-done.1), channel_id=1, replica_groups=mesh['row'=4,'col'=8] {'row'}, dimensions={0}, use_global_device_ids=true | all-gather | bytes 819200 | tf_op jit(solution)/shard_map/all_gather | solution.py:35
  65.7 14.4 %reduce-scatter.2.cloned.1.call-done = f32[32,2560]{1,0:T(8,128)} async-done(((f32[128,2560]{1,0:T(8,128)}), f32[32,2560]{1,0:T(8,128)}) %reduce-scatter.2.cloned.1.call-update) | async-done | bytes 327696 | tf_op jit(solution)/shard_map/reduce_scatter | solution.py:42
  80.1 1.0 reshape.87
  81.1 427.1 %scatter_custom_fusion = f32[36864]{0:T(1024)} fusion(s32[81920]{0:T(1024)S(1)} %reshape.85, f32[81920]{0:T(1024)S(1)} %reshape.87, f32[]{:T(128)} %constant.8.clone.1), kind=kCustom, calls=%fused_computation.5 | custom fusion | flops 81920 | bytes 147460 | tf_op jit(solution)/shard_map/scatter-add | solution.py:49
  508.2 0.0 all-reduce.3.cloned.1.call-update
  508.3 0.0 copy-done
  508.3 19.6 %subtract_convert_fusion = bf16[4608,2560]{1,0:T(8,128)(2,1)} fusion(bf16[4608,2560]{1,0:T(8,128)(2,1)} %param.11, bf16[128,4608]{1,0:T(8,128)(2,1)S(1)} %convolution_convert_fusion, bf16[128,2560]{1,0:T(8,128)(2,1)S(1)} %all_gather.11), kind=kOutput, calls=%fused_computation.2 | convolution fusion | flops 3055288320 | bytes 49020928 | tf_op jit(solution)/shard_map/dot_general | solution.py:33
  527.8 102.8 %all-reduce.3.cloned.1.call-done = f32[36864]{0:T(1024)} async-done(((f32[36864]{0:T(1024)}), f32[36864]{0:T(1024)}) %all-reduce.3.cloned.1.call-update) | async-done | bytes 147472
  630.6 1.4 dynamic-slice_multiply_fusion
  (4 shorter events, 0.0 us)
Async XLA Ops:
  7.2 28.0 %all-gather.2.cloned.1.call-start = ((), (), s32[]{:S(2)}) async-start(), calls=%async_computation.1 | async-start | bytes 1327104 | tf_op jit(solution)/shard_map/all_gather | solution.py:28
  7.9 72.2 %reduce-scatter.2.cloned.1.call-start = ((), (), s32[]{:S(2)}) async-start(), calls=%async_computation.2 | async-start | bytes 1638400 | tf_op jit(solution)/shard_map/reduce_scatter | solution.py:42
  36.9 471.3 %copy-start = (bf16[128,4608]{1,0:T(8,128)(2,1)}, bf16[128,4608]{1,0:T(8,128)(2,1)S(1)}, u32[]{:S(2)}) copy-start(bf16[128,4608]{1,0:T(8,128)(2,1)S(1)} %convolution_convert_fusion) | copy-start | bytes 3538948
  47.9 0.7 copy-start.3
  47.9 0.8 copy-start.4
  47.9 1.7 copy-start.2
  47.9 1.9 copy-start.1
  47.9 582.7 %all-reduce.3.cloned.1.call-start = ((), (), s32[]{:S(2)}) async-start(), calls=%async_computation.3 | async-start | bytes 294912
Sparse Core Ops, SparseCore 0:
  9.6 25.4 all-gather.1
  48.0 32.0 reduce-scatter.1
  508.4 122.2 all-reduce.2
where the time goes:
time: 640 us; the launch traced here: 639 us
  other arithmetic  429 us (67%)
  waiting for transfers between devices  129 us (20%)
  matrix products  32.3 us (5%)
  blocking collectives  31.8 us (5%)
  between operations  13.9 us (2%)
    scatter-add x1, other arithmetic, per_device(): jax.ops.segment_sum(correlation.reshape(-1), cell_index, num_segments=NDIAG)  427 us
    unnamed x4, waiting for transfers between devices  103 us
    dot_general x1, matrix products, per_device(): lax.dot_general(panel_adjoint, lax.all_gather(panel_factor, 'row', axis=0...  19.6 us
    all_gather x1, blocking collectives, per_device(): lax.all_gather(diag_inverse, 'col', axis=0, tiled=True)  15.9 us
    all_gather x1, blocking collectives, per_device(): lax.all_gather(panel_factor, 'row', axis=0, tiled=True)  15.9 us
    reduce_scatter x1, waiting for transfers between devices, per_device(): lax.psum_scatter(correlation, 'row', scatter_dimension=0, tiled=True)  14.4 us
  transfers between devices with their start and end apart: 3, of which 3 were waited for; matrix products, arithmetic and copies ran while one was open for 3% of the time, Pallas kernels for 0%

commit v1 on v0

v1 whole, which is shorter than its diff:
```python
import functools
import math

import jax
import jax.numpy as jnp
from jax import lax
from jax.experimental import pallas as pl
from jax.experimental.pallas import tpu as pltpu
from jax.sharding import PartitionSpec as P

NB = 128
S = 18432
ORDERS = 91
DPITCH = 192
NDIAG = 36864
LANES = 128
QUADS = (ORDERS + 3) // 4
XROWS = 4 * QUADS
ACCS = 8
BF = jnp.bfloat16
F32 = jnp.float32

FIRST = (((0,), (0,)), ((), ()))
WHOLE = pl.BlockSpec(memory_space=pltpu.VMEM)
SCALARS = pl.BlockSpec(memory_space=pltpu.SMEM)
ANYWHERE = pl.BlockSpec(memory_space=pl.ANY)


def bits_of(size):
    return [b for b in range(size.bit_length() - 1)]


def swap(x, axis, bit):
    size = lax.axis_size(axis)
    return lax.ppermute(x, axis, [(i, i ^ (1 << bit)) for i in range(size)])


def tile_of(size, options):
    return next(t for t in options if size % t == 0)


def correlate_kernel(chunk, inverse_ref, rhs_ref, field_ref, adjoint_ref, corr_ref, held, sem):
    count = rhs_ref.shape[1] // chunk
    copies = []
    for i in range(count):
        rows = pl.ds(i * chunk, chunk)
        copies.append(pltpu.make_async_copy(field_ref.at[rows], held.at[rows], sem.at[i]))
    for copy in copies:
        copy.start()
    for i in range(count):
        part = slice(i * chunk, (i + 1) * chunk)
        solved = lax.dot_general(
            inverse_ref[...], rhs_ref[:, part], FIRST, preferred_element_type=F32
        )
        adjoint_ref[:, part] = solved.astype(BF)
    for i in range(count):
        copies[i].wait()
        part = slice(i * chunk, (i + 1) * chunk)
        term = jnp.dot(adjoint_ref[:, part], held[part, :], preferred_element_type=F32)
        if i == 0:
            corr_ref[...] = term
        else:
            corr_ref[...] += term


def correlate(inverse, rhs, field):
    sources, cols = field.shape
    chunk = tile_of(sources, (256, 128))
    return pl.pallas_call(
        functools.partial(correlate_kernel, chunk),
        in_specs=[WHOLE, WHOLE, ANYWHERE],
        out_specs=[WHOLE, WHOLE],
        out_shape=[
            jax.ShapeDtypeStruct((NB, sources), BF),
            jax.ShapeDtypeStruct((NB, cols), F32),
        ],
        scratch_shapes=[
            pltpu.VMEM((sources, cols), BF),
            pltpu.SemaphoreType.DMA((sources // chunk,)),
        ],
        name="correlate",
    )(inverse, rhs, field)


def cells_kernel(pivot_ref, panel_ref, corr_ref, odd_ref, slot_ref, out_ref, left, grid, acc):
    corr = corr_ref[...]
    odd = odd_ref[...]
    left[0:NB, :] = jnp.where(odd == 0, corr, 0.0).astype(BF)
    left[NB : 2 * NB, :] = jnp.where(odd == 1, corr, 0.0).astype(BF)
    one, zero = jnp.ones((), BF), jnp.zeros((), BF)

    @pl.loop(0, QUADS)
    def _(n):
        slot = slot_ref[...]
        hot = [
            jnp.where(slot == (2 * n + h).astype(F32).astype(BF), one, zero) for h in range(2)
        ]
        placed = jnp.dot(left[...], jnp.concatenate(hot, axis=1), preferred_element_type=F32)
        for h in range(2):
            for g in range(2):
                grid[pl.ds((4 * n + 2 * h + g) * NB, NB), :] = placed[
                    g * NB : (g + 1) * NB, h * LANES : (h + 1) * LANES
                ]

    acc[...] = jnp.zeros_like(acc)
    lane = lax.broadcasted_iota(jnp.int32, (XROWS, LANES), 1)

    @pl.loop(0, NB // ACCS)
    def _(block):
        for u in range(ACCS):
            a = block * ACCS + u
            row = pivot_ref[a]
            hx, hy = panel_ref[0, row], panel_ref[1, row]
            patch = pltpu.roll(grid[pl.ds(a, XROWS, stride=NB), :], hy, axis=1)
            rows = pl.ds(hx, XROWS)
            acc[2 * u, rows, :] += jnp.where(lane >= hy, patch, 0.0)
            acc[2 * u + 1, rows, :] += jnp.where(lane < hy, patch, 0.0)

    for side in range(2):
        total = acc[side, :DPITCH, :]
        for u in range(1, ACCS):
            total = total + acc[2 * u + side, :DPITCH, :]
        out_ref[:, side * LANES : (side + 1) * LANES] = total


def cells(corr, pivot, panel_harmonic, odd, slot):
    cols = corr.shape[1]
    return pl.pallas_call(
        cells_kernel,
        in_specs=[SCALARS, SCALARS, WHOLE, WHOLE, WHOLE],
        out_specs=WHOLE,
        out_shape=jax.ShapeDtypeStruct((DPITCH, 2 * LANES), F32),
        scratch_shapes=[
            pltpu.VMEM((2 * NB, cols), BF),
            pltpu.VMEM((XROWS * NB, LANES), F32),
            pltpu.VMEM((2 * ACCS, DPITCH + 8, LANES), F32),
        ],
        name="cells",
    )(pivot, panel_harmonic, corr, odd, slot)


def update_kernel(adjoint_ref, factor_ref, trail_ref, *refs):
    out_ref = refs[-1]
    update = lax.dot_general(
        adjoint_ref[...], factor_ref[...], FIRST, preferred_element_type=F32
    )
    out_ref[...] = (trail_ref[...].astype(F32) - update).astype(BF)


def update_part(adjoint, factor, trail, before, tile, first, count):
    sources, cols = trail.shape
    wide = pl.BlockSpec((tile, cols), lambda i: (first + i, 0))
    specs = [
        pl.BlockSpec((NB, tile), lambda i: (0, first + i)),
        pl.BlockSpec((NB, cols), lambda i: (0, 0)),
        wide,
    ]
    operands = [adjoint, factor, trail]
    aliases = {}
    if before is not None:
        specs.append(ANYWHERE)
        operands.append(before)
        aliases = {3: 0}
    rows = tile * count
    return pl.pallas_call(
        update_kernel,
        grid=(count,),
        in_specs=specs,
        out_specs=wide,
        out_shape=jax.ShapeDtypeStruct((sources, cols), BF),
        input_output_aliases=aliases,
        cost_estimate=pl.CostEstimate(
            flops=2 * rows * cols * NB, bytes_accessed=4 * rows * cols, transcendentals=0
        ),
        name="update",
    )(*operands)


def per_device(
    panel_factor,
    diag_inverse,
    panel_rhs,
    trail_rhs,
    forward_field,
    pivot,
    panel_harmonic,
    trail_harmonic,
):
    cols_n, rows_n = lax.axis_size("col"), lax.axis_size("row")
    col, row = lax.axis_index("col"), lax.axis_index("row")

    mirror = (ORDERS - 1) - trail_harmonic
    odd = (mirror[0] % 2)[None, :]
    slot = jnp.where(
        mirror[1][:, None] == jnp.arange(LANES)[None, :], (mirror[0] // 2)[:, None], -1
    ).astype(BF)

    packed = jnp.concatenate([diag_inverse, panel_rhs], axis=1)
    for bit in reversed(bits_of(cols_n)):
        packed = jnp.concatenate([packed, swap(packed, "col", bit)], axis=0)
    inverse, rhs = packed[:, :NB], packed[:, NB:]

    factor = panel_factor
    for bit in bits_of(rows_n):
        factor = jnp.concatenate([factor, swap(factor, "row", bit)], axis=0)
    part = panel_factor.shape[0]
    factor = jnp.concatenate(
        [lax.dynamic_slice_in_dim(factor, (j ^ row) * part, part, 0) for j in range(rows_n)],
        axis=0,
    )

    adjoint, corr = correlate(inverse, rhs, forward_field)
    grad = cells(corr, pivot, panel_harmonic, odd, slot)

    tile = tile_of(trail_rhs.shape[0], (384, 128))
    tiles = trail_rhs.shape[0] // tile
    pieces = 4
    bounds = [tiles * k // pieces for k in range(pieces + 1)]
    trail_update = None
    for lo, hi in zip(bounds[:-1], bounds[1:]):
        if hi > lo:
            trail_update = update_part(
                adjoint, factor, trail_rhs, trail_update, tile, lo, hi - lo
            )

    share = NDIAG // (rows_n * cols_n)
    grad = grad[:, :DPITCH].reshape(rows_n, cols_n, share)
    for bit in bits_of(cols_n):
        mine = (col >> bit) & 1
        pairs = grad.reshape(grad.shape[0], grad.shape[1] // 2, 2, share)
        sent = lax.dynamic_index_in_dim(pairs, 1 - mine, 2, keepdims=False)
        kept = lax.dynamic_index_in_dim(pairs, mine, 2, keepdims=False)
        grad = kept + swap(sent, "col", bit)
    for bit in bits_of(rows_n):
        mine = (row >> bit) & 1
        pairs = grad.reshape(grad.shape[0] // 2, 2, 1, share)
        sent = lax.dynamic_index_in_dim(pairs, 1 - mine, 1, keepdims=False)
        kept = lax.dynamic_index_in_dim(pairs, mine, 1, keepdims=False)
        grad = kept + swap(sent, "row", bit)
    eps_grad = grad.reshape(-1) * jnp.float32(1.0 / math.sqrt(S * NB))
    return (adjoint, trail_update, eps_grad)


def solution(mesh):
    placed = (
        P("row", "col"),
        P("col", None),
        P("col", "row"),
        P("row", "col"),
        P("row", "col"),
        P(),
        P(),
        P(None, "col"),
    )
    return jax.shard_map(
        per_device,
        mesh=mesh,
        in_specs=placed,
        out_specs=(P(None, "row"), P("row", "col"), P(("row", "col"))),
        check_vma=False,
    )
```

time: 640 us -> 99.3 us (0.16)
  other arithmetic: 429 us -> 7.34 us
  waiting for transfers between devices: 129 us -> 8.85 us
  Pallas kernels: 0 us -> 61.2 us
  matrix products: 32.3 us -> 0 us
  blocking collectives: 31.8 us -> 0 us
  starting transfers between devices: 0.12 us -> 16.5 us
  between operations: 13.9 us -> 0.83 us
    scatter-add x1 -> x0, other arithmetic: 427 us -> none  [per_device(): jax.ops.segment_sum(correlation.reshape(-1), cell_index, num_segments=NDIAG)]
    unnamed x4 -> x0, waiting for transfers between devices: 103 us -> none
    pallas_call x0 -> x6, Pallas kernels: none -> 61.2 us  [the longest x4 29.8 us: update_part(): pl.pallas_call(update_kernel, grid=(count,), in_specs=specs, out_specs=wi...]
    dot_general x3 -> x0, matrix products: 32.3 us -> none  [the longest x1 19.6 us: per_device(): lax.dot_general(panel_adjoint, lax.all_gather(panel_factor, 'row', axis=0...]
    all_gather x2 -> x0, blocking collectives: 31.8 us -> none  [the longest x1 15.9 us: per_device(): lax.all_gather(diag_inverse, 'col', axis=0, tiled=True)]
    ppermute x0 -> x10, starting transfers between devices: none -> 16.5 us  [swap(): return lax.ppermute(x, axis, [(i, i ^ 1 << bit) for i in range(size)])]
    reduce_scatter x1 -> x0, waiting for transfers between devices: 14.4 us -> none  [per_device(): lax.psum_scatter(correlation, 'row', scatter_dimension=0, tiled=True)]
    all_gather x1 -> x0, waiting for transfers between devices: 11.3 us -> none  [per_device(): lax.all_gather(panel_rhs, 'col', axis=0, tiled=True)]
  transfers between devices with their start and end apart: 3 -> 10, of which waited for: 3 -> 5; matrix products, arithmetic and copies ran while one was open for 3% -> 6% of each run, Pallas kernels for 0% -> 30%
where the time goes in v1:
time: 99.3 us; the launch traced here: 98.8 us
  Pallas kernels  61.2 us (62%)
  starting transfers between devices  16.5 us (17%)
  waiting for transfers between devices  8.85 us (9%)
  other arithmetic  7.34 us (7%)
  local copies, waits for them, and re-layouts  4.12 us (4%)
    pallas_call x4, Pallas kernels, update_part(): pl.pallas_call(update_kernel, grid=(count,), in_specs=specs, out_specs=wi...  29.8 us
    pallas_call x1, Pallas kernels, cells(): pl.pallas_call(cells_kernel, in_specs=[SCALARS, SCALARS, WHOLE, WHOLE, WH...  20.8 us
    ppermute x10, starting transfers between devices, swap(): return lax.ppermute(x, axis, [(i, i ^ 1 << bit) for i in range(size)])  16.5 us
    pallas_call x1, Pallas kernels, correlate(): pl.pallas_call(functools.partial(correlate_kernel, chunk), in_specs=[WHOL...  10.7 us
    ppermute x10, waiting for transfers between devices, swap(): return lax.ppermute(x, axis, [(i, i ^ 1 << bit) for i in range(size)])  8.85 us
    convert_element_type x1, other arithmetic, per_device(): slot = jnp.where(mirror[1][:, None] == jnp.arange(LANES)[None, :], (mirro...  2.55 us
  transfers between devices with their start and end apart: 10, of which 5 were waited for; matrix products, arithmetic and copies ran while one was open for 6% of the time, Pallas kernels for 30%

profile of v1, /device:TPU:0, one launch (start us, length us, event | category | flops | bytes accessed | tf_op | source)
XLA Modules:
  0.0 98.8 jit_solution(1795064382534178851)
XLA Ops:
  0.6 0.0 copy-start
  0.6 0.7 constant_dynamic-update-slice_fusion.1
  1.4 0.9 constant_dynamic-update-slice_fusion
  2.3 4.1 %collective-permute-start = (bf16[16,4736]{1,0:T(8,128)(2,1)S(1)}, bf16[16,4736]{1,0:T(8,128)(2,1)S(1)}, u32[]{:S(2)}, u32[]{:S(2)}) collective-permute-start(bf16[16,4736]{1,0:T(8,128)(2,1)S(1)} %constant_dynamic-update-slice_fusion), channel_id=1, source_target_pairs={{0,4},{1,5},{2,6},{3,7},{4,0},{5,1},{6,2},{7,3},{8,12},{9,13},{10,... | collective-permute-start | bytes 454664 | tf_op jit(solution)/shard_map/ppermute | solution.py:35
  6.4 1.5 %collective-permute-start.3 = (bf16[32,2560]{1,0:T(8,128)(2,1)}, bf16[32,2560]{1,0:T(8,128)(2,1)S(1)}, u32[]{:S(2)}, u32[]{:S(2)}) collective-permute-start(bf16[32,2560]{1,0:T(8,128)(2,1)} %param.8), channel_id=1, source_target_pairs={{0,8},{8,0},{16,24},{24,16},{1,9},{9,1},{17,25},{25,17},{2,10},{10... | collective-permute-start | bytes 491528 | tf_op jit(solution)/shard_map/ppermute | solution.py:35
  7.9 0.7 broadcast_subtract_fusion
  8.7 0.6 slice_reduce_fusion
  9.3 2.5 %select_convert_fusion.slot_ref = bf16[2560,128]{1,0:T(8,128)(2,1)} fusion(s32[2560]{0:T(1024)S(1)} %add_select_fusion, s32[2560]{0:T(1024)S(1)} %get-tuple-element.7), kind=kLoop, calls=%fused_computation | loop fusion | flops 983040 | bytes 675840 | tf_op jit(solution)/shard_map/convert_element_type | solution.py:196
  11.9 0.9 constant_dynamic-update-slice_fusion.4
  12.8 0.8 collective-permute-done
  13.6 0.9 collective-permute-start.1
  14.5 0.0 collective-permute-done.3
  14.5 0.0 copy-done
  14.5 1.6 %collective-permute-start.4 = (bf16[64,2560]{1,0:T(8,128)(2,1)S(1)}, bf16[64,2560]{1,0:T(8,128)(2,1)S(1)}, u32[]{:S(2)}, u32[]{:S(2)}) collective-permute-start(bf16[64,2560]{1,0:T(8,128)(2,1)S(1)} %pad_maximum_fusion.5), channel_id=1, source_target_pairs={{0,16},{8,24},{16,0},{24,8},{1,17},{9,25},{17,1},{25,9},{2,18},{10... | collective-permute-start | bytes 983048 | tf_op jit(solution)/shard_map/ppermute | solution.py:35
  16.1 5.9 %collective-permute-done.1 = bf16[32,4736]{1,0:T(8,128)(2,1)S(1)} collective-permute-done((bf16[32,4736]{1,0:T(8,128)(2,1)S(1)}, bf16[32,4736]{1,0:T(8,128)(2,1)S(1)}, u32[]{:S(2)}, u32[]{:S(2)}) %collective-permute-start.1) | collective-permute-done | bytes 303136 | tf_op jit(solution)/shard_map/ppermute | solution.py:35
  22.0 0.1 pad_maximum_fusion.4
  22.1 0.1 collective-permute-start.2
  22.2 1.7 %collective-permute-done.4 = bf16[64,2560]{1,0:T(8,128)(2,1)S(1)} collective-permute-done((bf16[64,2560]{1,0:T(8,128)(2,1)S(1)}, bf16[64,2560]{1,0:T(8,128)(2,1)S(1)}, u32[]{:S(2)}, u32[]{:S(2)}) %collective-permute-start.4) | collective-permute-done | bytes 327712 | tf_op jit(solution)/shard_map/ppermute | solution.py:35
  23.9 0.1 constant_dynamic-slice_fusion.9
  24.0 0.2 collective-permute-done.2
  24.2 0.6 pad_maximum_fusion.7.inverse_ref
  24.8 1.1 %pad_maximum_fusion.rhs_ref = bf16[128,4608]{1,0:T(8,128)(2,1)} fusion(bf16[64,4736]{1,0:T(8,128)(2,1)S(1)} %collective-permute-done.2, bf16[32,4736]{1,0:T(8,128)(2,1)S(1)} %collective-permute-done.1, bf16[16,4736]{1,0:T(8,128)(2,1)S(1)} %collective-permute-done, bf16[16,4736]{1,0:T(8,128)(2,1)S(1)} %constant_dynamic-update-slice_fusion), kind=kLoop, calls=%fused_computation.2 | loop fusion | flops 4718592 | bytes 2392064 | tf_op jit(solution)/shard_map/concatenate | solution.py:200
  25.9 10.7 %correlate.1 = (bf16[128,4608]{1,0:T(8,128)(2,1)}, f32[128,2560]{1,0:T(8,128)}) custom-call(bf16[128,128]{1,0:T(8,128)(2,1)} %pad_maximum_fusion.7.inverse_ref, bf16[128,4608]{1,0:T(8,128)(2,1)} %pad_maximum_fusion.rhs_ref, bf16[4608,2560]{1,0:T(8,128)(2,1)} %field_ref.1), custom_call_target="tpu_custom_call" | custom-call | tf_op jit(solution)/shard_map/correlate/pallas_call | solution.py:69
  36.6 20.8 %cells.1 = f32[192,256]{1,0:T(8,128)} custom-call(s32[128]{0:T(128)} %pivot_ref.1, s32[2,128]{1,0:T(2,128)} %panel_ref.1, f32[128,2560]{1,0:T(8,128)} %get-tuple-element.6.corr_ref, s32[1,2560]{1,0:T(1,128)} %get-tuple-element.17.odd_ref, bf16[2560,128]{1,0:T(8,128)(2,1)} %select_convert_fusion.slot_ref), custom_call_target="tpu_custom_call" | custom-call | tf_op jit(solution)/shard_map/cells/pallas_call | solution.py:128
  57.4 1.1 %reshape_reshape.3 = f32[4,4,2,1152]{3,2,1,0:T(2,128)S(1)} reshape(f32[192,192]{1,0:T(8,128)} %bitcast.16) | data formatting | bytes 294912 | tf_op jit(solution)/shard_map/reshape;reshape | solution.py:230
  58.5 0.1 constant_dynamic-slice_fusion.5
  58.6 0.2 collective-permute-start.5
  58.8 0.9 pad_maximum_fusion.3.factor_ref
  59.7 0.2 collective-permute-done.5
  60.0 0.1 reshape.54
  60.1 0.1 constant_dynamic-slice_fusion.3
  60.2 1.5 %collective-permute-start.6 = (f32[4,2,1152]{2,1,0:T(2,128)S(1)}, f32[4,2,1152]{2,1,0:T(2,128)S(1)}, u32[]{:S(2)}, u32[]{:S(2)}) collective-permute-start(f32[4,2,1152]{2,1,0:T(2,128)S(1)} %bitcast.20), channel_id=1, source_target_pairs={{0,2},{1,3},{2,0},{3,1},{4,6},{5,7},{6,4},{7,5},{8,10},{9,11},{10,... | collective-permute-start | bytes 110600 | tf_op jit(solution)/shard_map/ppermute | solution.py:35
  61.7 7.5 %update.4.refs_0_ = bf16[4608,2560]{1,0:T(8,128)(2,1)} custom-call(bf16[128,4608]{1,0:T(8,128)(2,1)} %get-tuple-element.2.adjoint_ref, bf16[128,2560]{1,0:T(8,128)(2,1)} %pad_maximum_fusion.3.factor_ref, bf16[4608,2560]{1,0:T(8,128)(2,1)} %trail_ref.7), custom_call_target="tpu_custom_call" | custom-call | flops 754974720 | bytes 11796480 | tf_op jit(solution)/shard_map/update/pallas_call | solution.py:165
  69.2 0.0 collective-permute-done.6
  69.2 3.4 %collective-permute-start.7 = (f32[4,1,1152]{2,1,0:T(1,128)S(1)}, f32[4,1,1152]{2,1,0:T(1,128)S(1)}, u32[]{:S(2)}, u32[]{:S(2)}) collective-permute-start(f32[4,1,1152]{2,1,0:T(1,128)S(1)} %constant_dynamic-slice_fusion.1), channel_id=1, source_target_pairs={{0,4},{1,5},{2,6},{3,7},{4,0},{5,1},{6,2},{7,3},{8,12},{9,13},{10,... | collective-permute-start | bytes 55304 | tf_op jit(solution)/shard_map/ppermute | solution.py:35
  72.7 7.4 %update.5.refs_0_ = bf16[4608,2560]{1,0:T(8,128)(2,1)} custom-call(bf16[128,4608]{1,0:T(8,128)(2,1)} %get-tuple-element.2.adjoint_ref, bf16[128,2560]{1,0:T(8,128)(2,1)} %pad_maximum_fusion.3.factor_ref, bf16[4608,2560]{1,0:T(8,128)(2,1)} %trail_ref.7, bf16[4608,2560]{1,0:T(8,128)(2,1)} %update.4.refs_0_), custom_call_target="tpu_custom_call", output_to_operand_aliasing={{}: (3, {})} | custom-call | flops 754974720 | bytes 11796480 | tf_op jit(solution)/shard_map/update/pallas_call | solution.py:165
  80.1 0.0 collective-permute-done.7
  80.2 1.6 %collective-permute-start.8 = (f32[2,1,1152]{2,1,0:T(1,128)S(1)}, f32[2,1,1152]{2,1,0:T(1,128)S(1)}, u32[]{:S(2)}, u32[]{:S(2)}) collective-permute-start(f32[2,1,1152]{2,1,0:T(1,128)S(1)} %dynamic-slice_bitcast_fusion), channel_id=1, source_target_pairs={{0,8},{8,0},{16,24},{24,16},{1,9},{9,1},{17,25},{25,17},{2,10},{10... | collective-permute-start | bytes 27656 | tf_op jit(solution)/shard_map/ppermute | solution.py:35
  81.7 7.4 %update.6.refs_0_ = bf16[4608,2560]{1,0:T(8,128)(2,1)} custom-call(bf16[128,4608]{1,0:T(8,128)(2,1)} %get-tuple-element.2.adjoint_ref, bf16[128,2560]{1,0:T(8,128)(2,1)} %pad_maximum_fusion.3.factor_ref, bf16[4608,2560]{1,0:T(8,128)(2,1)} %trail_ref.7, bf16[4608,2560]{1,0:T(8,128)(2,1)} %update.5.refs_0_), custom_call_target="tpu_custom_call", output_to_operand_aliasing={{}: (3, {})} | custom-call | flops 754974720 | bytes 11796480 | tf_op jit(solution)/shard_map/update/pallas_call | solution.py:165
  89.2 0.0 collective-permute-done.8
  89.2 1.6 %collective-permute-start.9 = (f32[1,1,1152]{2,1,0:T(1,128)S(1)}, f32[1,1,1152]{2,1,0:T(1,128)S(1)}, u32[]{:S(2)}, u32[]{:S(2)}) collective-permute-start(f32[1,1,1152]{2,1,0:T(1,128)S(1)} %constant_dynamic-slice_fusion), channel_id=1, source_target_pairs={{0,16},{8,24},{16,0},{24,8},{1,17},{9,25},{17,1},{25,9},{2,18},{10... | collective-permute-start | bytes 13832 | tf_op jit(solution)/shard_map/ppermute | solution.py:35
  90.8 7.4 %update.7 = bf16[4608,2560]{1,0:T(8,128)(2,1)} custom-call(bf16[128,4608]{1,0:T(8,128)(2,1)} %get-tuple-element.2.adjoint_ref, bf16[128,2560]{1,0:T(8,128)(2,1)} %pad_maximum_fusion.3.factor_ref, bf16[4608,2560]{1,0:T(8,128)(2,1)} %trail_ref.7, bf16[4608,2560]{1,0:T(8,128)(2,1)} %update.6.refs_0_), custom_call_target="tpu_custom_call", output_to_operand_aliasing={{}: (3, {})} | custom-call | flops 754974720 | bytes 11796480 | tf_op jit(solution)/shard_map/update/pallas_call | solution.py:165
  98.2 0.0 collective-permute-done.9
  98.2 0.6 multiply_reduce_fusion
  (14 shorter events, 0.3 us)
Async XLA Ops:
  0.6 13.9 %copy-start = (bf16[32,2560]{1,0:T(8,128)(2,1)S(1)}, bf16[32,2560]{1,0:T(8,128)(2,1)}, u32[]{:S(2)}) copy-start(bf16[32,2560]{1,0:T(8,128)(2,1)} %param.8) | copy-start | bytes 491524
  2.3 11.3 %collective-permute-start = (bf16[16,4736]{1,0:T(8,128)(2,1)S(1)}, bf16[16,4736]{1,0:T(8,128)(2,1)S(1)}, u32[]{:S(2)}, u32[]{:S(2)}) collective-permute-start(bf16[16,4736]{1,0:T(8,128)(2,1)S(1)} %constant_dynamic-update-slice_fusion), channel_id=1, source_target_pairs={{0,4},{1,5},{2,6},{3,7},{4,0},{5,1},{6,2},{7,3},{8,12},{9,13},{10,... | collective-permute-start | bytes 454664 | tf_op jit(solution)/shard_map/ppermute | solution.py:35
  6.4 8.1 %collective-permute-start.3 = (bf16[32,2560]{1,0:T(8,128)(2,1)}, bf16[32,2560]{1,0:T(8,128)(2,1)S(1)}, u32[]{:S(2)}, u32[]{:S(2)}) collective-permute-start(bf16[32,2560]{1,0:T(8,128)(2,1)} %param.8), channel_id=1, source_target_pairs={{0,8},{8,0},{16,24},{24,16},{1,9},{9,1},{17,25},{25,17},{2,10},{10... | collective-permute-start | bytes 491528 | tf_op jit(solution)/shard_map/ppermute | solution.py:35
  13.6 8.4 %collective-permute-start.1 = (bf16[32,4736]{1,0:T(8,128)(2,1)S(1)}, bf16[32,4736]{1,0:T(8,128)(2,1)S(1)}, u32[]{:S(2)}, u32[]{:S(2)}) collective-permute-start(bf16[32,4736]{1,0:T(8,128)(2,1)S(1)} %pad_maximum_fusion.6), channel_id=1, source_target_pairs={{0,2},{1,3},{2,0},{3,1},{4,6},{5,7},{6,4},{7,5},{8,10},{9,11},{10,... | collective-permute-start | bytes 909320 | tf_op jit(solution)/shard_map/ppermute | solution.py:35
  14.5 9.3 %collective-permute-start.4 = (bf16[64,2560]{1,0:T(8,128)(2,1)S(1)}, bf16[64,2560]{1,0:T(8,128)(2,1)S(1)}, u32[]{:S(2)}, u32[]{:S(2)}) collective-permute-start(bf16[64,2560]{1,0:T(8,128)(2,1)S(1)} %pad_maximum_fusion.5), channel_id=1, source_target_pairs={{0,16},{8,24},{16,0},{24,8},{1,17},{9,25},{17,1},{25,9},{2,18},{10... | collective-permute-start | bytes 983048 | tf_op jit(solution)/shard_map/ppermute | solution.py:35
  22.1 2.1 %collective-permute-start.2 = (bf16[64,4736]{1,0:T(8,128)(2,1)S(1)}, bf16[64,4736]{1,0:T(8,128)(2,1)S(1)}, u32[]{:S(2)}, u32[]{:S(2)}) collective-permute-start(bf16[64,4736]{1,0:T(8,128)(2,1)S(1)} %pad_maximum_fusion.4), channel_id=1, source_target_pairs={{0,1},{1,0},{2,3},{3,2},{4,5},{5,4},{6,7},{7,6},{8,9},{9,8},{10,11... | collective-permute-start | bytes 1818632 | tf_op jit(solution)/shard_map/ppermute | solution.py:35
  58.6 1.3 %collective-permute-start.5 = (f32[4,4,1152]{2,1,0:T(4,128)S(1)}, f32[4,4,1152]{2,1,0:T(4,128)S(1)}, u32[]{:S(2)}, u32[]{:S(2)}) collective-permute-start(f32[4,4,1152]{2,1,0:T(4,128)S(1)} %bitcast.19), channel_id=1, source_target_pairs={{0,1},{1,0},{2,3},{3,2},{4,5},{5,4},{6,7},{7,6},{8,9},{9,8},{10,11... | collective-permute-start | bytes 221192 | tf_op jit(solution)/shard_map/ppermute | solution.py:35
  60.2 9.0 %collective-permute-start.6 = (f32[4,2,1152]{2,1,0:T(2,128)S(1)}, f32[4,2,1152]{2,1,0:T(2,128)S(1)}, u32[]{:S(2)}, u32[]{:S(2)}) collective-permute-start(f32[4,2,1152]{2,1,0:T(2,128)S(1)} %bitcast.20), channel_id=1, source_target_pairs={{0,2},{1,3},{2,0},{3,1},{4,6},{5,7},{6,4},{7,5},{8,10},{9,11},{10,... | collective-permute-start | bytes 110600 | tf_op jit(solution)/shard_map/ppermute | solution.py:35
  69.2 10.9 %collective-permute-start.7 = (f32[4,1,1152]{2,1,0:T(1,128)S(1)}, f32[4,1,1152]{2,1,0:T(1,128)S(1)}, u32[]{:S(2)}, u32[]{:S(2)}) collective-permute-start(f32[4,1,1152]{2,1,0:T(1,128)S(1)} %constant_dynamic-slice_fusion.1), channel_id=1, source_target_pairs={{0,4},{1,5},{2,6},{3,7},{4,0},{5,1},{6,2},{7,3},{8,12},{9,13},{10,... | collective-permute-start | bytes 55304 | tf_op jit(solution)/shard_map/ppermute | solution.py:35
  80.2 9.0 %collective-permute-start.8 = (f32[2,1,1152]{2,1,0:T(1,128)S(1)}, f32[2,1,1152]{2,1,0:T(1,128)S(1)}, u32[]{:S(2)}, u32[]{:S(2)}) collective-permute-start(f32[2,1,1152]{2,1,0:T(1,128)S(1)} %dynamic-slice_bitcast_fusion), channel_id=1, source_target_pairs={{0,8},{8,0},{16,24},{24,16},{1,9},{9,1},{17,25},{25,17},{2,10},{10... | collective-permute-start | bytes 27656 | tf_op jit(solution)/shard_map/ppermute | solution.py:35
  89.2 9.0 %collective-permute-start.9 = (f32[1,1,1152]{2,1,0:T(1,128)S(1)}, f32[1,1,1152]{2,1,0:T(1,128)S(1)}, u32[]{:S(2)}, u32[]{:S(2)}) collective-permute-start(f32[1,1,1152]{2,1,0:T(1,128)S(1)} %constant_dynamic-slice_fusion), channel_id=1, source_target_pairs={{0,16},{8,24},{16,0},{24,8},{1,17},{9,25},{17,1},{25,9},{2,18},{10... | collective-permute-start | bytes 13832 | tf_op jit(solution)/shard_map/ppermute | solution.py:35
